TPU v7x, 128 devices: a whole 4x4x4 slice. The times are simulated.
128 devices in a mesh: ao: 8 (over y, x_hi), prow: 8 (over z, core), pcol: 2 (over x_lo).
Axes of the slice: x: 4 (x_hi: 2, x_lo: 2; x = x_hi * 2 + x_lo), y: 4, z: 4, core: 2. Of those that a mesh axis runs over, the one named last changes fastest.
Arguments:
- three_index: bfloat16 [1024, 1200, 1200], P(('prow', 'pcol'), 'ao'), may hold values from -1.0546875 to 1.0546875
- coefficients: bfloat16 [1200, 120], replicated, may hold values from -0.1875 to 0.1875
Outputs:
- coulomb: bfloat16 [14400, 14400], P('ao', ('prow', 'pcol'))
All inputs are finite; a program needn't handle non-finite values.
Results may differ from a plain program's by a relative error of at most 0.0069.
Values may be sent and summed in bfloat16 or wider, within the bound.
No kernel may reach another device: no remote copies, remote signals or barrier semaphores. Data moves between devices by JAX's collectives and lax.ppermute only.
A program may use at most 192 MiB of HBM per device.

v0:
```python
import functools

import jax
import jax.numpy as jnp
from jax import lax
from jax.experimental import pallas as pl
from jax.experimental.pallas import tpu as pltpu
from jax.sharding import PartitionSpec as P


AXES = ("ao", "prow", "pcol")
STEPS = (2, 1, 3)
SLOTS = (
    ((0, 0), (0, 1), (2, 0), (2, 1), (1, 0), (1, 1), (3, 0), (3, 1)),
    ((0, 0), (2, 0), (0, 1), (2, 1), (3, 1), (1, 1), (3, 0), (1, 0)),
)


def place():
    ao, prow = lax.axis_index("ao"), lax.axis_index("prow")
    return ao // 2, lax.rem(ao, 2), prow // 2, lax.rem(prow, 2), lax.axis_index("pcol")


def send(value, to):
    pairs = []
    for y in range(4):
        for xh in range(2):
            for z in range(4):
                for k in range(2):
                    for xl in range(2):
                        y2, xh2, z2, k2, xl2 = to(y, xh, z, k, xl)
                        source = ((y * 2 + xh) * 8 + z * 2 + k) * 2 + xl
                        target = ((y2 % 4 * 2 + xh2 % 2) * 8 + z2 % 4 * 2 + k2 % 2) * 2 + xl2 % 2
                        pairs.append((source, target))
    return lax.ppermute(value, AXES, pairs)


def pairs_kernel(block_ref, coef_ref, *rest, rows, group, active, per, steps):
    outs, (half_a, half_b, ints, wide_coef, own) = rest[:4], rest[4:]
    y, xh, _, core, _ = place()
    basis = block_ref.shape[2]
    step = pl.program_id(0)

    @pl.when(step == 0)
    def _():
        wide_coef[:basis, :active] = coef_ref[...].astype(jnp.float32)
        mine = wide_coef[pl.ds((2 * y + xh) * rows, 256), :]
        own[...] = mine.T[:active, :rows].astype(jnp.bfloat16)

    def first(half):
        half[:, :active] = jnp.dot(
            block_ref[...].reshape(rows * group, basis),
            coef_ref[...],
            preferred_element_type=jnp.float32,
        )

    def second(half):
        wide = jnp.concatenate(
            [half[pl.ds(p, rows, stride=group), :].astype(jnp.bfloat16) for p in range(group)],
            axis=1,
        )
        product = jnp.dot(own[...], wide, preferred_element_type=jnp.float32)
        for p in range(group):
            ints[p * active : (p + 1) * active, :] = product[:, p * 128 : (p + 1) * 128]
        for slot in range(8):
            (dy0, dx0), (dy1, dx1) = SLOTS[0][slot], SLOTS[1][slot]
            dy = dy0 + core * (dy1 - dy0)
            dx = dx0 + core * (dx1 - dx0)
            start = (lax.rem(y + dy, 4) * 2 + lax.rem(xh + dx, 2)) * per
            pieces = [ints[pl.ds(start + j, group, stride=active), :][:, :active] for j in range(per)]
            outs[slot // 2][slot % 2] = jnp.concatenate(pieces, axis=1).astype(jnp.bfloat16)

    even = lax.rem(step, 2) == 0

    @pl.when(step == 0)
    def _():
        first(half_a)

    @pl.when((step > 0) & (step < steps) & jnp.logical_not(even))
    def _():
        first(half_b)
        second(half_a)

    @pl.when((step > 0) & (step < steps) & even)
    def _():
        first(half_a)
        second(half_b)

    @pl.when(step == steps)
    def _():
        second(half_b if steps % 2 == 0 else half_a)


def pair_terms(three_index, coefficients, group=16):
    block = jnp.transpose(three_index, (1, 0, 2))
    rows, aux, basis = block.shape
    active = coefficients.shape[1]
    per = active // 8
    steps = aux // group
    message = jax.ShapeDtypeStruct((2, aux, per * active), jnp.bfloat16)
    half = pltpu.VMEM((rows * group, 128), jnp.float32)
    return pl.pallas_call(
        functools.partial(
            pairs_kernel, rows=rows, group=group, active=active, per=per, steps=steps
        ),
        out_shape=(message,) * 4,
        grid=(steps + 1,),
        in_specs=[
            pl.BlockSpec((rows, group, basis), lambda i: (0, jnp.minimum(i, steps - 1), 0)),
            pl.BlockSpec((basis, active), lambda i: (0, 0), pipeline_mode=pl.Buffered(1)),
        ],
        out_specs=(
            pl.BlockSpec((2, group, per * active), lambda i: (0, jnp.maximum(i - 1, 0), 0)),
        )
        * 4,
        scratch_shapes=[
            half,
            half,
            pltpu.VMEM((group * active, 128), jnp.float32),
            pltpu.VMEM((7 * rows + 256 + 6, 128), jnp.float32),
            pltpu.VMEM((active, rows), jnp.bfloat16),
        ],
        compiler_params=pltpu.CompilerParams(vmem_limit_bytes=32 << 20),
        name="pair_terms",
    )(block, coefficients)


def sum_scatter(messages):
    f32 = lambda v: v.astype(jnp.float32)
    core = lax.rem(lax.axis_index("prow"), 2)

    def first(j):
        def to(y, xh, z, k, xl):
            if k == 0:
                return y + STEPS[j], xh, z, k, xl
            return y, xh + (j < 2), z, k, xl

        return to

    def second(j):
        def to(y, xh, z, k, xl):
            if k == 1:
                return y + STEPS[j], xh, z, k, xl
            return y, xh + (j < 1), z, k, xl

        return to

    got = [send(messages[j + 1], first(j)) for j in range(3)]
    near = f32(messages[0]) + f32(got[0])
    near = jnp.where(core == 0, near + f32(got[1]) + f32(got[2]), near)
    far = f32(messages[3]) + f32(got[1])
    got = [
        send(near[1].astype(jnp.bfloat16), second(0)),
        send(far[1].astype(jnp.bfloat16), second(1)),
        send(far[0].astype(jnp.bfloat16), second(2)),
    ]
    total = near[0] + f32(got[0])
    return jnp.where(core == 0, total, total + f32(got[1]) + f32(got[2])).astype(jnp.bfloat16)


def row_panel(block):
    across = send(block, lambda y, xh, z, k, xl: (y, xh, z, k, xl + 1))
    mine = {(0, 0): block, (0, 1): across}
    for flip, piece in ((0, block), (1, across)):
        for d in STEPS[flip:]:
            mine[d, flip] = send(piece, lambda y, xh, z, k, xl, d=d: (y, xh, z + d, k, xl))
    mine[2, 1] = send(mine[2, 0], lambda y, xh, z, k, xl: (y, xh, z, k, xl + 1))
    twins = []
    for d, flip in sorted(mine):
        twins.append(send(mine[d, flip], lambda y, xh, z, k, xl: (y, xh, z, k + 1, xl)))
    return [mine[key] for key in sorted(mine)] + twins


def column_panel(block):
    width = block.shape[1] // 2
    xl = lax.axis_index("pcol")
    left, right = block[:, :width], block[:, width:]
    same = send(
        jnp.where(xl == 0, left, right), lambda y, xh, z, k, xl: (2 * y - z + 2, k, y, xh, xl)
    )
    other = send(
        jnp.where(xl == 0, right, left), lambda y, xh, z, k, xl: (2 * y - z + 2, k, y, xh, xl + 1)
    )
    both = jnp.stack([same, other])
    across = send(both, lambda y, xh, z, k, xl: (y, xh + 1, z, k, xl))
    mine = {(0, 0): both, (0, 1): across}
    for flip, piece in ((0, both), (1, across)):
        for d in STEPS[flip:]:
            mine[d, flip] = send(piece, lambda y, xh, z, k, xl, d=d: (y + d, xh, z, k, xl))
    mine[2, 1] = send(mine[2, 0], lambda y, xh, z, k, xl: (y, xh + 1, z, k, xl))
    return [mine[key] for key in sorted(mine)]


def product_kernel(*refs, tile):
    row_refs, col_refs = refs[:16], refs[16:24]
    out_ref, cols, stage, out_sem = refs[24:]
    y, xh, z, k, _ = place()
    where = [(d, flip) for d in range(4) for flip in range(2)]
    for ref, (d, flip) in zip(col_refs, where):
        base = 2 * lax.rem(y + 6 - d - z, 4) + 8 * lax.rem(xh + flip + k, 2)
        for j in range(2):
            cols[base + j] = ref[j]
    _, aux, width = cols.shape
    right = jnp.concatenate([ref[...] for ref in row_refs], axis=0)
    stores = []
    for t, start in enumerate(range(0, width, tile)):
        stop = min(start + tile, width)
        left = cols[:, :, start:stop].reshape(16 * aux, stop - start)
        stage[start:stop] = lax.dot_general(
            left, right, (((0,), (0,)), ((), ())), preferred_element_type=jnp.float32
        ).astype(jnp.bfloat16)
        stores.append(
            pltpu.make_async_copy(stage.at[start:stop], out_ref.at[start:stop], out_sem.at[t])
        )
        stores[-1].start()
    for store in stores:
        store.wait()


def product(rows, cols, tile=256):
    aux, height = rows[0].shape
    width = cols[0].shape[2]
    inside = pl.BlockSpec(memory_space=pltpu.VMEM)
    return pl.pallas_call(
        functools.partial(product_kernel, tile=tile),
        out_shape=jax.ShapeDtypeStruct((width, height), jnp.bfloat16),
        in_specs=[inside] * (len(rows) + len(cols)),
        out_specs=pl.BlockSpec(memory_space=pl.ANY),
        scratch_shapes=[
            pltpu.VMEM((16, aux, width), jnp.bfloat16),
            pltpu.VMEM((width, height), jnp.bfloat16),
            pltpu.SemaphoreType.DMA((-(-width // tile),)),
        ],
        compiler_params=pltpu.CompilerParams(vmem_limit_bytes=32 << 20),
        name="product",
    )(*rows, *cols).T


def on_device(three_index, coefficients):
    block = sum_scatter(pair_terms(three_index, coefficients))
    return product(row_panel(block), column_panel(block))


def solution(mesh):
    placed = (P(("prow", "pcol"), "ao", None), P())
    return jax.shard_map(
        on_device, mesh=mesh, in_specs=placed, out_specs=P("ao", ("prow", "pcol")), check_vma=False
    )
```

profile of v0, /device:TPU:1, one launch (start us, length us, event | category | flops | bytes accessed | tf_op | source)
XLA Modules:
  0.0 100.9 jit_solution(11123594558565887524)
XLA Ops:
  1.0 13.2 %pair_terms.1 = (bf16[2,64,1800]{2,1,0:T(8,128)(2,1)S(1)}, bf16[2,64,1800]{2,1,0:T(8,128)(2,1)S(1)}, bf16[2,64,1800]{2,1,0:T(8,128)(2,1)S(1)}, bf16[2,64,1800]{2,1,0:T(8,128)(2,1)S(1)}) custom-call(bf16[150,64,1200]{2,1,0:T(8,128)(2,1)} %bitcast.16, bf16[1200,120]{1,0:T(8,128)(2,1)S(1)} %copy-done), custom_call_target="tpu_custom_call" | custom-call | tf_op jit(solution)/shard_map/pair_terms/pallas_call | solution.py:102
  14.2 3.6 %collective-permute-start = (bf16[2,64,1800]{2,1,0:T(8,128)(2,1)S(1)}, bf16[2,64,1800]{2,1,0:T(8,128)(2,1)S(1)}, u32[]{:S(2)}, u32[]{:S(2)}) collective-permute-start(bf16[2,64,1800]{2,1,0:T(8,128)(2,1)S(1)} %get-tuple-element.10), channel_id=1, source_target_pairs={{0,64},{1,65},{2,18},{3,19},{4,68},{5,69},{6,22},{7,23},{8,72},{9,... | collective-permute-start | bytes 1382408 | tf_op jit(solution)/shard_map/ppermute | solution.py:35
  18.6 5.7 %collective-permute-done = bf16[2,64,1800]{2,1,0:T(8,128)(2,1)S(1)} collective-permute-done((bf16[2,64,1800]{2,1,0:T(8,128)(2,1)S(1)}, bf16[2,64,1800]{2,1,0:T(8,128)(2,1)S(1)}, u32[]{:S(2)}, u32[]{:S(2)}) %collective-permute-start) | collective-permute-done | bytes 460832 | tf_op jit(solution)/shard_map/ppermute | solution.py:35
  24.3 5.0 %collective-permute-done.1 = bf16[2,64,1800]{2,1,0:T(8,128)(2,1)S(1)} collective-permute-done((bf16[2,64,1800]{2,1,0:T(8,128)(2,1)S(1)}, bf16[2,64,1800]{2,1,0:T(8,128)(2,1)S(1)}, u32[]{:S(2)}, u32[]{:S(2)}) %collective-permute-start.1) | collective-permute-done | bytes 460832 | tf_op jit(solution)/shard_map/ppermute | solution.py:35
  29.7 3.2 %collective-permute-start.3 = (bf16[64,1800]{1,0:T(8,128)(2,1)S(1)}, bf16[64,1800]{1,0:T(8,128)(2,1)S(1)}, u32[]{:S(2)}, u32[]{:S(2)}) collective-permute-start(bf16[64,1800]{1,0:T(8,128)(2,1)S(1)} %fusion.4), channel_id=1, source_target_pairs={{0,16},{1,17},{2,66},{3,67},{4,20},{5,21},{6,70},{7,71},{8,24},{9,... | collective-permute-start | bytes 691208 | tf_op jit(solution)/shard_map/ppermute | solution.py:35
  32.9 2.3 %collective-permute-start.4 = (bf16[64,1800]{1,0:T(8,128)(2,1)S(1)}, bf16[64,1800]{1,0:T(8,128)(2,1)S(1)}, u32[]{:S(2)}, u32[]{:S(2)}) collective-permute-start(bf16[64,1800]{1,0:T(8,128)(2,1)S(1)} %get-tuple-element.13), channel_id=1, source_target_pairs={{0,0},{1,1},{2,34},{3,35},{4,4},{5,5},{6,38},{7,39},{8,8},{9,9},{1... | collective-permute-start | bytes 691208 | tf_op jit(solution)/shard_map/ppermute | solution.py:35
  35.2 4.2 %collective-permute-start.5 = (bf16[64,1800]{1,0:T(8,128)(2,1)S(1)}, bf16[64,1800]{1,0:T(8,128)(2,1)S(1)}, u32[]{:S(2)}, u32[]{:S(2)}) collective-permute-start(bf16[64,1800]{1,0:T(8,128)(2,1)S(1)} %get-tuple-element.14), channel_id=1, source_target_pairs={{0,0},{1,1},{2,98},{3,99},{4,4},{5,5},{6,102},{7,103},{8,8},{9,9},... | collective-permute-start | bytes 691208 | tf_op jit(solution)/shard_map/ppermute | solution.py:35
  39.5 1.6 %collective-permute-done.4 = bf16[64,1800]{1,0:T(8,128)(2,1)S(1)} collective-permute-done((bf16[64,1800]{1,0:T(8,128)(2,1)S(1)}, bf16[64,1800]{1,0:T(8,128)(2,1)S(1)}, u32[]{:S(2)}, u32[]{:S(2)}) %collective-permute-start.4) | collective-permute-done | bytes 230432 | tf_op jit(solution)/shard_map/ppermute | solution.py:35
  41.1 1.5 %collective-permute-done.5 = bf16[64,1800]{1,0:T(8,128)(2,1)S(1)} collective-permute-done((bf16[64,1800]{1,0:T(8,128)(2,1)S(1)}, bf16[64,1800]{1,0:T(8,128)(2,1)S(1)}, u32[]{:S(2)}, u32[]{:S(2)}) %collective-permute-start.5) | collective-permute-done | bytes 230432 | tf_op jit(solution)/shard_map/ppermute | solution.py:35
  42.8 1.6 %collective-permute-start.21 = (bf16[64,900]{1,0:T(8,128)(2,1)S(1)}, bf16[64,900]{1,0:T(8,128)(2,1)S(1)}, u32[]{:S(2)}, u32[]{:S(2)}) collective-permute-start(bf16[64,900]{1,0:T(8,128)(2,1)S(1)} %get-tuple-element.17), channel_id=1, source_target_pairs={{0,64},{1,65},{2,80},{3,81},{4,32},{5,33},{6,48},{7,49},{8,0},{9,1... | collective-permute-start | bytes 345608 | tf_op jit(solution)/shard_map/ppermute | solution.py:35
  44.4 7.1 %collective-permute-start.22 = (bf16[64,900]{1,0:T(8,128)(2,1)S(1)}, bf16[64,900]{1,0:T(8,128)(2,1)S(1)}, u32[]{:S(2)}, u32[]{:S(2)}) collective-permute-start(bf16[64,900]{1,0:T(8,128)(2,1)S(1)} %get-tuple-element.18), channel_id=1, source_target_pairs={{0,65},{1,64},{2,81},{3,80},{4,33},{5,32},{6,49},{7,48},{8,1},{9,0... | collective-permute-start | bytes 345608 | tf_op jit(solution)/shard_map/ppermute | solution.py:35
  51.4 3.7 %collective-permute-start.11 = (bf16[64,1800]{1,0:T(8,128)(2,1)S(1)}, bf16[64,1800]{1,0:T(8,128)(2,1)S(1)}, u32[]{:S(2)}, u32[]{:S(2)}) collective-permute-start(bf16[64,1800]{1,0:T(8,128)(2,1)S(1)} %select_convert_fusion.refs_0_), channel_id=1, source_target_pairs={{0,12},{1,13},{2,14},{3,15},{4,0},{5,1},{6,2},{7,3},{8,4},{9,5},{1... | collective-permute-start | bytes 691208 | tf_op jit(solution)/shard_map/ppermute | solution.py:35
  55.7 5.1 %collective-permute-start.28 = (bf16[2,64,900]{2,1,0:T(8,128)(2,1)S(1)}, bf16[2,64,900]{2,1,0:T(8,128)(2,1)S(1)}, u32[]{:S(2)}, u32[]{:S(2)}) collective-permute-start(bf16[2,64,900]{2,1,0:T(8,128)(2,1)S(1)} %pad_maximum_fusion.refs_16_), channel_id=1, source_target_pairs={{0,96},{1,97},{2,98},{3,99},{4,100},{5,101},{6,102},{7,103},{8,104... | collective-permute-start | bytes 691208 | tf_op jit(solution)/shard_map/ppermute | solution.py:35
  60.8 4.4 %collective-permute-done.11.refs_6_ = bf16[64,1800]{1,0:T(8,128)(2,1)S(1)} collective-permute-done((bf16[64,1800]{1,0:T(8,128)(2,1)S(1)}, bf16[64,1800]{1,0:T(8,128)(2,1)S(1)}, u32[]{:S(2)}, u32[]{:S(2)}) %collective-permute-start.11) | collective-permute-done | bytes 230432 | tf_op jit(solution)/shard_map/ppermute | solution.py:35
  65.2 4.0 %collective-permute-done.7.refs_2_ = bf16[64,1800]{1,0:T(8,128)(2,1)S(1)} collective-permute-done((bf16[64,1800]{1,0:T(8,128)(2,1)S(1)}, bf16[64,1800]{1,0:T(8,128)(2,1)S(1)}, u32[]{:S(2)}, u32[]{:S(2)}) %collective-permute-start.7) | collective-permute-done | bytes 230432 | tf_op jit(solution)/shard_map/ppermute | solution.py:35
  70.3 2.9 %collective-permute-done.26.refs_20_ = bf16[2,64,900]{2,1,0:T(8,128)(2,1)S(1)} collective-permute-done((bf16[2,64,900]{2,1,0:T(8,128)(2,1)S(1)}, bf16[2,64,900]{2,1,0:T(8,128)(2,1)S(1)}, u32[]{:S(2)}, u32[]{:S(2)}) %collective-permute-start.26) | collective-permute-done | bytes 230432 | tf_op jit(solution)/shard_map/ppermute | solution.py:35
  73.3 1.3 %collective-permute-start.10 = (bf16[64,1800]{1,0:T(8,128)(2,1)S(1)}, bf16[64,1800]{1,0:T(8,128)(2,1)S(1)}, u32[]{:S(2)}, u32[]{:S(2)}) collective-permute-start(bf16[64,1800]{1,0:T(8,128)(2,1)S(1)} %collective-permute-done.9.refs_4_), channel_id=1, source_target_pairs={{0,1},{1,0},{2,3},{3,2},{4,5},{5,4},{6,7},{7,6},{8,9},{9,8},{10,11... | collective-permute-start | bytes 691208 | tf_op jit(solution)/shard_map/ppermute | solution.py:35
  74.6 5.4 %collective-permute-done.24.refs_18_ = bf16[2,64,900]{2,1,0:T(8,128)(2,1)S(1)} collective-permute-done((bf16[2,64,900]{2,1,0:T(8,128)(2,1)S(1)}, bf16[2,64,900]{2,1,0:T(8,128)(2,1)S(1)}, u32[]{:S(2)}, u32[]{:S(2)}) %collective-permute-start.24) | collective-permute-done | bytes 230432 | tf_op jit(solution)/shard_map/ppermute | solution.py:35
  80.7 3.5 %collective-permute-start.12 = (bf16[64,1800]{1,0:T(8,128)(2,1)S(1)}, bf16[64,1800]{1,0:T(8,128)(2,1)S(1)}, u32[]{:S(2)}, u32[]{:S(2)}) collective-permute-start(bf16[64,1800]{1,0:T(8,128)(2,1)S(1)} %collective-permute-done.6.refs_1_), channel_id=1, source_target_pairs={{0,12},{1,13},{2,14},{3,15},{4,0},{5,1},{6,2},{7,3},{8,4},{9,5},{1... | collective-permute-start | bytes 691208 | tf_op jit(solution)/shard_map/ppermute | solution.py:35
  84.2 2.9 %collective-permute-start.27 = (bf16[2,64,900]{2,1,0:T(8,128)(2,1)S(1)}, bf16[2,64,900]{2,1,0:T(8,128)(2,1)S(1)}, u32[]{:S(2)}, u32[]{:S(2)}) collective-permute-start(bf16[2,64,900]{2,1,0:T(8,128)(2,1)S(1)} %collective-permute-done.26.refs_20_), channel_id=1, source_target_pairs={{0,16},{1,17},{2,18},{3,19},{4,20},{5,21},{6,22},{7,23},{8,24},{9,... | collective-permute-start | bytes 691208 | tf_op jit(solution)/shard_map/ppermute | solution.py:35
  89.1 1.3 %collective-permute-start.18 = (bf16[64,1800]{1,0:T(8,128)(2,1)S(1)}, bf16[64,1800]{1,0:T(8,128)(2,1)S(1)}, u32[]{:S(2)}, u32[]{:S(2)}) collective-permute-start(bf16[64,1800]{1,0:T(8,128)(2,1)S(1)} %collective-permute-done.10.refs_5_), channel_id=1, source_target_pairs={{0,2},{1,3},{2,0},{3,1},{4,6},{5,7},{6,4},{7,5},{8,10},{9,11},{10,... | collective-permute-start | bytes 691208 | tf_op jit(solution)/shard_map/ppermute | solution.py:35
  90.4 1.8 %collective-permute-done.8.refs_3_ = bf16[64,1800]{1,0:T(8,128)(2,1)S(1)} collective-permute-done((bf16[64,1800]{1,0:T(8,128)(2,1)S(1)}, bf16[64,1800]{1,0:T(8,128)(2,1)S(1)}, u32[]{:S(2)}, u32[]{:S(2)}) %collective-permute-start.8) | collective-permute-done | bytes 230432 | tf_op jit(solution)/shard_map/ppermute | solution.py:35
  92.2 1.6 %collective-permute-start.20 = (bf16[64,1800]{1,0:T(8,128)(2,1)S(1)}, bf16[64,1800]{1,0:T(8,128)(2,1)S(1)}, u32[]{:S(2)}, u32[]{:S(2)}) collective-permute-start(bf16[64,1800]{1,0:T(8,128)(2,1)S(1)} %collective-permute-done.12.refs_7_), channel_id=1, source_target_pairs={{0,2},{1,3},{2,0},{3,1},{4,6},{5,7},{6,4},{7,5},{8,10},{9,11},{10,... | collective-permute-start | bytes 691208 | tf_op jit(solution)/shard_map/ppermute | solution.py:35
  95.7 5.0 %product.1 = bf16[900,1800]{1,0:T(8,128)(2,1)} custom-call(bf16[64,1800]{1,0:T(8,128)(2,1)S(1)} %select_convert_fusion.refs_0_, bf16[64,1800]{1,0:T(8,128)(2,1)S(1)} %collective-permute-done.6.refs_1_, bf16[64,1800]{1,0:T(8,128)(2,1)S(1)} %collective-permute-done.7.refs_2_, bf16[64,1800]{1,0:T(8,128)(2,1)S(1)} %collective-permute-done.8.refs_3_, ...), custom_call_target="tpu_custom_call" | custom-call | tf_op jit(solution)/shard_map/product/pallas_call | solution.py:224
  (46 shorter events, 8.8 us)
Async XLA Ops:
  14.2 10.1 %collective-permute-start = (bf16[2,64,1800]{2,1,0:T(8,128)(2,1)S(1)}, bf16[2,64,1800]{2,1,0:T(8,128)(2,1)S(1)}, u32[]{:S(2)}, u32[]{:S(2)}) collective-permute-start(bf16[2,64,1800]{2,1,0:T(8,128)(2,1)S(1)} %get-tuple-element.10), channel_id=1, source_target_pairs={{0,64},{1,65},{2,18},{3,19},{4,68},{5,69},{6,22},{7,23},{8,72},{9,... | collective-permute-start | bytes 1382408 | tf_op jit(solution)/shard_map/ppermute | solution.py:35
  17.8 11.5 %collective-permute-start.1 = (bf16[2,64,1800]{2,1,0:T(8,128)(2,1)S(1)}, bf16[2,64,1800]{2,1,0:T(8,128)(2,1)S(1)}, u32[]{:S(2)}, u32[]{:S(2)}) collective-permute-start(bf16[2,64,1800]{2,1,0:T(8,128)(2,1)S(1)} %get-tuple-element.11), channel_id=1, source_target_pairs={{0,32},{1,33},{2,18},{3,19},{4,36},{5,37},{6,22},{7,23},{8,40},{9,... | collective-permute-start | bytes 1382408 | tf_op jit(solution)/shard_map/ppermute | solution.py:35
  17.9 11.4 %collective-permute-start.2 = (bf16[2,64,1800]{2,1,0:T(8,128)(2,1)S(1)}, bf16[2,64,1800]{2,1,0:T(8,128)(2,1)S(1)}, u32[]{:S(2)}, u32[]{:S(2)}) collective-permute-start(bf16[2,64,1800]{2,1,0:T(8,128)(2,1)S(1)} %get-tuple-element.12), channel_id=1, source_target_pairs={{0,96},{1,97},{2,2},{3,3},{4,100},{5,101},{6,6},{7,7},{8,104},{9,1... | collective-permute-start | bytes 1382408 | tf_op jit(solution)/shard_map/ppermute | solution.py:35
  29.7 9.7 %collective-permute-start.3 = (bf16[64,1800]{1,0:T(8,128)(2,1)S(1)}, bf16[64,1800]{1,0:T(8,128)(2,1)S(1)}, u32[]{:S(2)}, u32[]{:S(2)}) collective-permute-start(bf16[64,1800]{1,0:T(8,128)(2,1)S(1)} %fusion.4), channel_id=1, source_target_pairs={{0,16},{1,17},{2,66},{3,67},{4,20},{5,21},{6,70},{7,71},{8,24},{9,... | collective-permute-start | bytes 691208 | tf_op jit(solution)/shard_map/ppermute | solution.py:35
  32.9 8.1 %collective-permute-start.4 = (bf16[64,1800]{1,0:T(8,128)(2,1)S(1)}, bf16[64,1800]{1,0:T(8,128)(2,1)S(1)}, u32[]{:S(2)}, u32[]{:S(2)}) collective-permute-start(bf16[64,1800]{1,0:T(8,128)(2,1)S(1)} %get-tuple-element.13), channel_id=1, source_target_pairs={{0,0},{1,1},{2,34},{3,35},{4,4},{5,5},{6,38},{7,39},{8,8},{9,9},{1... | collective-permute-start | bytes 691208 | tf_op jit(solution)/shard_map/ppermute | solution.py:35
  35.2 7.3 %collective-permute-start.5 = (bf16[64,1800]{1,0:T(8,128)(2,1)S(1)}, bf16[64,1800]{1,0:T(8,128)(2,1)S(1)}, u32[]{:S(2)}, u32[]{:S(2)}) collective-permute-start(bf16[64,1800]{1,0:T(8,128)(2,1)S(1)} %get-tuple-element.14), channel_id=1, source_target_pairs={{0,0},{1,1},{2,98},{3,99},{4,4},{5,5},{6,102},{7,103},{8,8},{9,9},... | collective-permute-start | bytes 691208 | tf_op jit(solution)/shard_map/ppermute | solution.py:35
  42.8 12.3 %collective-permute-start.21 = (bf16[64,900]{1,0:T(8,128)(2,1)S(1)}, bf16[64,900]{1,0:T(8,128)(2,1)S(1)}, u32[]{:S(2)}, u32[]{:S(2)}) collective-permute-start(bf16[64,900]{1,0:T(8,128)(2,1)S(1)} %get-tuple-element.17), channel_id=1, source_target_pairs={{0,64},{1,65},{2,80},{3,81},{4,32},{5,33},{6,48},{7,49},{8,0},{9,1... | collective-permute-start | bytes 345608 | tf_op jit(solution)/shard_map/ppermute | solution.py:35
  44.4 11.3 %collective-permute-start.22 = (bf16[64,900]{1,0:T(8,128)(2,1)S(1)}, bf16[64,900]{1,0:T(8,128)(2,1)S(1)}, u32[]{:S(2)}, u32[]{:S(2)}) collective-permute-start(bf16[64,900]{1,0:T(8,128)(2,1)S(1)} %get-tuple-element.18), channel_id=1, source_target_pairs={{0,65},{1,64},{2,81},{3,80},{4,33},{5,32},{6,49},{7,48},{8,1},{9,0... | collective-permute-start | bytes 345608 | tf_op jit(solution)/shard_map/ppermute | solution.py:35
  51.4 13.7 %collective-permute-start.11 = (bf16[64,1800]{1,0:T(8,128)(2,1)S(1)}, bf16[64,1800]{1,0:T(8,128)(2,1)S(1)}, u32[]{:S(2)}, u32[]{:S(2)}) collective-permute-start(bf16[64,1800]{1,0:T(8,128)(2,1)S(1)} %select_convert_fusion.refs_0_), channel_id=1, source_target_pairs={{0,12},{1,13},{2,14},{3,15},{4,0},{5,1},{6,2},{7,3},{8,4},{9,5},{1... | collective-permute-start | bytes 691208 | tf_op jit(solution)/shard_map/ppermute | solution.py:35
  55.1 10.1 %collective-permute-start.9 = (bf16[64,1800]{1,0:T(8,128)(2,1)S(1)}, bf16[64,1800]{1,0:T(8,128)(2,1)S(1)}, u32[]{:S(2)}, u32[]{:S(2)}) collective-permute-start(bf16[64,1800]{1,0:T(8,128)(2,1)S(1)} %select_convert_fusion.refs_0_), channel_id=1, source_target_pairs={{0,8},{1,9},{2,10},{3,11},{4,12},{5,13},{6,14},{7,15},{8,0},{9,1},... | collective-permute-start | bytes 691208 | tf_op jit(solution)/shard_map/ppermute | solution.py:35
  55.1 14.1 %collective-permute-start.7 = (bf16[64,1800]{1,0:T(8,128)(2,1)S(1)}, bf16[64,1800]{1,0:T(8,128)(2,1)S(1)}, u32[]{:S(2)}, u32[]{:S(2)}) collective-permute-start(bf16[64,1800]{1,0:T(8,128)(2,1)S(1)} %select_convert_fusion.refs_0_), channel_id=1, source_target_pairs={{0,4},{1,5},{2,6},{3,7},{4,8},{5,9},{6,10},{7,11},{8,12},{9,13},{1... | collective-permute-start | bytes 691208 | tf_op jit(solution)/shard_map/ppermute | solution.py:35
  55.7 13.8 %collective-permute-start.6 = (bf16[64,1800]{1,0:T(8,128)(2,1)S(1)}, bf16[64,1800]{1,0:T(8,128)(2,1)S(1)}, u32[]{:S(2)}, u32[]{:S(2)}) collective-permute-start(bf16[64,1800]{1,0:T(8,128)(2,1)S(1)} %select_convert_fusion.refs_0_), channel_id=1, source_target_pairs={{0,1},{1,0},{2,3},{3,2},{4,5},{5,4},{6,7},{7,6},{8,9},{9,8},{10,11... | collective-permute-start | bytes 691208 | tf_op jit(solution)/shard_map/ppermute | solution.py:35
  55.7 14.5 %collective-permute-start.28 = (bf16[2,64,900]{2,1,0:T(8,128)(2,1)S(1)}, bf16[2,64,900]{2,1,0:T(8,128)(2,1)S(1)}, u32[]{:S(2)}, u32[]{:S(2)}) collective-permute-start(bf16[2,64,900]{2,1,0:T(8,128)(2,1)S(1)} %pad_maximum_fusion.refs_16_), channel_id=1, source_target_pairs={{0,96},{1,97},{2,98},{3,99},{4,100},{5,101},{6,102},{7,103},{8,104... | collective-permute-start | bytes 691208 | tf_op jit(solution)/shard_map/ppermute | solution.py:35
  65.2 8.1 %collective-permute-start.26 = (bf16[2,64,900]{2,1,0:T(8,128)(2,1)S(1)}, bf16[2,64,900]{2,1,0:T(8,128)(2,1)S(1)}, u32[]{:S(2)}, u32[]{:S(2)}) collective-permute-start(bf16[2,64,900]{2,1,0:T(8,128)(2,1)S(1)} %pad_maximum_fusion.refs_16_), channel_id=1, source_target_pairs={{0,64},{1,65},{2,66},{3,67},{4,68},{5,69},{6,70},{7,71},{8,72},{9,... | collective-permute-start | bytes 691208 | tf_op jit(solution)/shard_map/ppermute | solution.py:35
  65.2 14.8 %collective-permute-start.24 = (bf16[2,64,900]{2,1,0:T(8,128)(2,1)S(1)}, bf16[2,64,900]{2,1,0:T(8,128)(2,1)S(1)}, u32[]{:S(2)}, u32[]{:S(2)}) collective-permute-start(bf16[2,64,900]{2,1,0:T(8,128)(2,1)S(1)} %pad_maximum_fusion.refs_16_), channel_id=1, source_target_pairs={{0,32},{1,33},{2,34},{3,35},{4,36},{5,37},{6,38},{7,39},{8,40},{9,... | collective-permute-start | bytes 691208 | tf_op jit(solution)/shard_map/ppermute | solution.py:35
  69.2 11.6 %collective-permute-start.23 = (bf16[2,64,900]{2,1,0:T(8,128)(2,1)S(1)}, bf16[2,64,900]{2,1,0:T(8,128)(2,1)S(1)}, u32[]{:S(2)}, u32[]{:S(2)}) collective-permute-start(bf16[2,64,900]{2,1,0:T(8,128)(2,1)S(1)} %pad_maximum_fusion.refs_16_), channel_id=1, source_target_pairs={{0,16},{1,17},{2,18},{3,19},{4,20},{5,21},{6,22},{7,23},{8,24},{9,... | collective-permute-start | bytes 691208 | tf_op jit(solution)/shard_map/ppermute | solution.py:35
  69.5 11.2 %collective-permute-start.19 = (bf16[64,1800]{1,0:T(8,128)(2,1)S(1)}, bf16[64,1800]{1,0:T(8,128)(2,1)S(1)}, u32[]{:S(2)}, u32[]{:S(2)}) collective-permute-start(bf16[64,1800]{1,0:T(8,128)(2,1)S(1)} %collective-permute-done.11.refs_6_), channel_id=1, source_target_pairs={{0,2},{1,3},{2,0},{3,1},{4,6},{5,7},{6,4},{7,5},{8,10},{9,11},{10,... | collective-permute-start | bytes 691208 | tf_op jit(solution)/shard_map/ppermute | solution.py:35
  70.2 14.0 %collective-permute-start.17 = (bf16[64,1800]{1,0:T(8,128)(2,1)S(1)}, bf16[64,1800]{1,0:T(8,128)(2,1)S(1)}, u32[]{:S(2)}, u32[]{:S(2)}) collective-permute-start(bf16[64,1800]{1,0:T(8,128)(2,1)S(1)} %collective-permute-done.9.refs_4_), channel_id=1, source_target_pairs={{0,2},{1,3},{2,0},{3,1},{4,6},{5,7},{6,4},{7,5},{8,10},{9,11},{10,... | collective-permute-start | bytes 691208 | tf_op jit(solution)/shard_map/ppermute | solution.py:35
  73.3 11.0 %collective-permute-start.10 = (bf16[64,1800]{1,0:T(8,128)(2,1)S(1)}, bf16[64,1800]{1,0:T(8,128)(2,1)S(1)}, u32[]{:S(2)}, u32[]{:S(2)}) collective-permute-start(bf16[64,1800]{1,0:T(8,128)(2,1)S(1)} %collective-permute-done.9.refs_4_), channel_id=1, source_target_pairs={{0,1},{1,0},{2,3},{3,2},{4,5},{5,4},{6,7},{7,6},{8,9},{9,8},{10,11... | collective-permute-start | bytes 691208 | tf_op jit(solution)/shard_map/ppermute | solution.py:35
  80.7 8.4 %collective-permute-start.12 = (bf16[64,1800]{1,0:T(8,128)(2,1)S(1)}, bf16[64,1800]{1,0:T(8,128)(2,1)S(1)}, u32[]{:S(2)}, u32[]{:S(2)}) collective-permute-start(bf16[64,1800]{1,0:T(8,128)(2,1)S(1)} %collective-permute-done.6.refs_1_), channel_id=1, source_target_pairs={{0,12},{1,13},{2,14},{3,15},{4,0},{5,1},{6,2},{7,3},{8,4},{9,5},{1... | collective-permute-start | bytes 691208 | tf_op jit(solution)/shard_map/ppermute | solution.py:35
  84.2 8.0 %collective-permute-start.8 = (bf16[64,1800]{1,0:T(8,128)(2,1)S(1)}, bf16[64,1800]{1,0:T(8,128)(2,1)S(1)}, u32[]{:S(2)}, u32[]{:S(2)}) collective-permute-start(bf16[64,1800]{1,0:T(8,128)(2,1)S(1)} %collective-permute-done.6.refs_1_), channel_id=1, source_target_pairs={{0,4},{1,5},{2,6},{3,7},{4,8},{5,9},{6,10},{7,11},{8,12},{9,13},{1... | collective-permute-start | bytes 691208 | tf_op jit(solution)/shard_map/ppermute | solution.py:35
  84.2 9.6 %collective-permute-start.27 = (bf16[2,64,900]{2,1,0:T(8,128)(2,1)S(1)}, bf16[2,64,900]{2,1,0:T(8,128)(2,1)S(1)}, u32[]{:S(2)}, u32[]{:S(2)}) collective-permute-start(bf16[2,64,900]{2,1,0:T(8,128)(2,1)S(1)} %collective-permute-done.26.refs_20_), channel_id=1, source_target_pairs={{0,16},{1,17},{2,18},{3,19},{4,20},{5,21},{6,22},{7,23},{8,24},{9,... | collective-permute-start | bytes 691208 | tf_op jit(solution)/shard_map/ppermute | solution.py:35
  87.2 7.4 %collective-permute-start.29 = (bf16[2,64,900]{2,1,0:T(8,128)(2,1)S(1)}, bf16[2,64,900]{2,1,0:T(8,128)(2,1)S(1)}, u32[]{:S(2)}, u32[]{:S(2)}) collective-permute-start(bf16[2,64,900]{2,1,0:T(8,128)(2,1)S(1)} %collective-permute-done.23.refs_17_), channel_id=1, source_target_pairs={{0,96},{1,97},{2,98},{3,99},{4,100},{5,101},{6,102},{7,103},{8,104... | collective-permute-start | bytes 691208 | tf_op jit(solution)/shard_map/ppermute | solution.py:35
  87.8 7.8 %collective-permute-start.25 = (bf16[2,64,900]{2,1,0:T(8,128)(2,1)S(1)}, bf16[2,64,900]{2,1,0:T(8,128)(2,1)S(1)}, u32[]{:S(2)}, u32[]{:S(2)}) collective-permute-start(bf16[2,64,900]{2,1,0:T(8,128)(2,1)S(1)} %collective-permute-done.23.refs_17_), channel_id=1, source_target_pairs={{0,32},{1,33},{2,34},{3,35},{4,36},{5,37},{6,38},{7,39},{8,40},{9,... | collective-permute-start | bytes 691208 | tf_op jit(solution)/shard_map/ppermute | solution.py:35
  (7 other events, 31.2 us)
where the time goes:
time: 102 us; the launch traced here: 101 us
  starting transfers between devices  46.7 us (46%)
  waiting for transfers between devices  33.9 us (33%)
  Pallas kernels  18.3 us (18%)
  local copies, waits for them, and re-layouts  1.03 us (1%)
    ppermute x30, starting transfers between devices, send(): return lax.ppermute(value, AXES, pairs)  46.7 us
    ppermute x30, waiting for transfers between devices, send(): return lax.ppermute(value, AXES, pairs)  33.9 us
    pallas_call x1, Pallas kernels, pair_terms(): pl.pallas_call(functools.partial(pairs_kernel, rows=rows, group=group, ac...  13.2 us
    pallas_call x1, Pallas kernels, product(): pl.pallas_call(functools.partial(product_kernel, tile=tile), out_shape=ja...  5.05 us
  transfers between devices with their start and end apart: 30, of which 12 were waited for; matrix products, arithmetic and copies ran while one was open for 0% of the time, Pallas kernels for 0%

commit v1 on v0

--- a/solution.py
+++ b/solution.py
@@ -122,7 +122,7 @@
         ],
         compiler_params=pltpu.CompilerParams(vmem_limit_bytes=32 << 20),
         name="pair_terms",
-    )(block, coefficients)
+    )(block, pltpu.with_memory_space_constraint(coefficients, pltpu.HBM))
 
 
 def sum_scatter(messages):
@@ -175,12 +175,18 @@
     width = block.shape[1] // 2
     xl = lax.axis_index("pcol")
     left, right = block[:, :width], block[:, width:]
-    same = send(
-        jnp.where(xl == 0, left, right), lambda y, xh, z, k, xl: (2 * y - z + 2, k, y, xh, xl)
-    )
-    other = send(
-        jnp.where(xl == 0, right, left), lambda y, xh, z, k, xl: (2 * y - z + 2, k, y, xh, xl + 1)
-    )
+    core = lax.rem(lax.axis_index("prow"), 2)
+    keep = xl == core
+
+    def turn(first):
+        def to(y, xh, z, k, xl):
+            flip = (k + first) % 2
+            return 2 * y - z + 2, xh + flip, y, xh, xl + flip
+
+        return to
+
+    same = send(jnp.where(keep, left, right), turn(0))
+    other = send(jnp.where(keep, right, left), turn(1))
     both = jnp.stack([same, other])
     across = send(both, lambda y, xh, z, k, xl: (y, xh + 1, z, k, xl))
     mine = {(0, 0): both, (0, 1): across}
@@ -197,9 +203,10 @@
     y, xh, z, k, _ = place()
     where = [(d, flip) for d in range(4) for flip in range(2)]
     for ref, (d, flip) in zip(col_refs, where):
-        base = 2 * lax.rem(y + 6 - d - z, 4) + 8 * lax.rem(xh + flip + k, 2)
+        kind = lax.rem(xh + flip + k, 2)
+        base = 2 * lax.rem(y + 6 - d - z, 4) + kind
         for j in range(2):
-            cols[base + j] = ref[j]
+            cols[base + 8 * lax.rem(j + kind + k, 2)] = ref[j]
     _, aux, width = cols.shape
     right = jnp.concatenate([ref[...] for ref in row_refs], axis=0)
     stores = []
@@ -217,7 +224,7 @@
         store.wait()
 
 
-def product(rows, cols, tile=256):
+def product(rows, cols, tile=384):
     aux, height = rows[0].shape
     width = cols[0].shape[2]
     inside = pl.BlockSpec(memory_space=pltpu.VMEM)

time: 102 us -> 100 us (0.980)
  starting transfers between devices: 46.7 us -> 44.4 us
  waiting for transfers between devices: 33.9 us -> 36.1 us
    ppermute x30, starting transfers between devices: 46.7 us -> 44.4 us  [send(): return lax.ppermute(value, AXES, pairs)]
    ppermute x30, waiting for transfers between devices: 33.9 us -> 36.1 us  [send(): return lax.ppermute(value, AXES, pairs)]
  transfers between devices with their start and end apart: 30 -> 30, of which waited for: 12 -> 13; matrix products, arithmetic and copies ran while one was open for 0% -> 0% of each run, Pallas kernels for 0% -> 0%
where the time goes in v1:
time: 100 us; the launch traced here: 99.6 us
  starting transfers between devices  44.4 us (44%)
  waiting for transfers between devices  36.1 us (36%)
  Pallas kernels  18.2 us (18%)
    ppermute x30, starting transfers between devices, send(): return lax.ppermute(value, AXES, pairs)  44.4 us
    ppermute x30, waiting for transfers between devices, send(): return lax.ppermute(value, AXES, pairs)  36.1 us
    pallas_call x1, Pallas kernels, pair_terms(): pl.pallas_call(functools.partial(pairs_kernel, rows=rows, group=group, ac...  13.2 us
    pallas_call x1, Pallas kernels, product(): pl.pallas_call(functools.partial(product_kernel, tile=tile), out_shape=ja...  5.03 us
  transfers between devices with their start and end apart: 30, of which 13 were waited for; matrix products, arithmetic and copies ran while one was open for 0% of the time, Pallas kernels for 0%

profile of v1, /device:TPU:1, one launch (start us, length us, event | category | flops | bytes accessed | tf_op | source)
XLA Modules:
  0.0 99.6 jit_solution(9104526524290454957)
XLA Ops:
  0.0 13.2 %pair_terms.1 = (bf16[2,64,1800]{2,1,0:T(8,128)(2,1)S(1)}, bf16[2,64,1800]{2,1,0:T(8,128)(2,1)S(1)}, bf16[2,64,1800]{2,1,0:T(8,128)(2,1)S(1)}, bf16[2,64,1800]{2,1,0:T(8,128)(2,1)S(1)}) custom-call(bf16[150,64,1200]{2,1,0:T(8,128)(2,1)} %bitcast.16, bf16[1200,120]{1,0:T(8,128)(2,1)} %coef_ref.1), custom_call_target="tpu_custom_call" | custom-call | tf_op jit(solution)/shard_map/pair_terms/pallas_call | solution.py:102
  13.2 3.6 %collective-permute-start = (bf16[2,64,1800]{2,1,0:T(8,128)(2,1)S(1)}, bf16[2,64,1800]{2,1,0:T(8,128)(2,1)S(1)}, u32[]{:S(2)}, u32[]{:S(2)}) collective-permute-start(bf16[2,64,1800]{2,1,0:T(8,128)(2,1)S(1)} %get-tuple-element.10), channel_id=1, source_target_pairs={{0,64},{1,65},{2,18},{3,19},{4,68},{5,69},{6,22},{7,23},{8,72},{9,... | collective-permute-start | bytes 1382408 | tf_op jit(solution)/shard_map/ppermute | solution.py:35
  17.6 5.7 %collective-permute-done = bf16[2,64,1800]{2,1,0:T(8,128)(2,1)S(1)} collective-permute-done((bf16[2,64,1800]{2,1,0:T(8,128)(2,1)S(1)}, bf16[2,64,1800]{2,1,0:T(8,128)(2,1)S(1)}, u32[]{:S(2)}, u32[]{:S(2)}) %collective-permute-start) | collective-permute-done | bytes 460832 | tf_op jit(solution)/shard_map/ppermute | solution.py:35
  23.4 5.0 %collective-permute-done.1 = bf16[2,64,1800]{2,1,0:T(8,128)(2,1)S(1)} collective-permute-done((bf16[2,64,1800]{2,1,0:T(8,128)(2,1)S(1)}, bf16[2,64,1800]{2,1,0:T(8,128)(2,1)S(1)}, u32[]{:S(2)}, u32[]{:S(2)}) %collective-permute-start.1) | collective-permute-done | bytes 460832 | tf_op jit(solution)/shard_map/ppermute | solution.py:35
  28.8 3.2 %collective-permute-start.3 = (bf16[64,1800]{1,0:T(8,128)(2,1)S(1)}, bf16[64,1800]{1,0:T(8,128)(2,1)S(1)}, u32[]{:S(2)}, u32[]{:S(2)}) collective-permute-start(bf16[64,1800]{1,0:T(8,128)(2,1)S(1)} %fusion.4), channel_id=1, source_target_pairs={{0,16},{1,17},{2,66},{3,67},{4,20},{5,21},{6,70},{7,71},{8,24},{9,... | collective-permute-start | bytes 691208 | tf_op jit(solution)/shard_map/ppermute | solution.py:35
  32.0 2.3 %collective-permute-start.4 = (bf16[64,1800]{1,0:T(8,128)(2,1)S(1)}, bf16[64,1800]{1,0:T(8,128)(2,1)S(1)}, u32[]{:S(2)}, u32[]{:S(2)}) collective-permute-start(bf16[64,1800]{1,0:T(8,128)(2,1)S(1)} %get-tuple-element.13), channel_id=1, source_target_pairs={{0,0},{1,1},{2,34},{3,35},{4,4},{5,5},{6,38},{7,39},{8,8},{9,9},{1... | collective-permute-start | bytes 691208 | tf_op jit(solution)/shard_map/ppermute | solution.py:35
  34.3 4.2 %collective-permute-start.5 = (bf16[64,1800]{1,0:T(8,128)(2,1)S(1)}, bf16[64,1800]{1,0:T(8,128)(2,1)S(1)}, u32[]{:S(2)}, u32[]{:S(2)}) collective-permute-start(bf16[64,1800]{1,0:T(8,128)(2,1)S(1)} %get-tuple-element.14), channel_id=1, source_target_pairs={{0,0},{1,1},{2,98},{3,99},{4,4},{5,5},{6,102},{7,103},{8,8},{9,9},... | collective-permute-start | bytes 691208 | tf_op jit(solution)/shard_map/ppermute | solution.py:35
  38.5 1.6 %collective-permute-done.4 = bf16[64,1800]{1,0:T(8,128)(2,1)S(1)} collective-permute-done((bf16[64,1800]{1,0:T(8,128)(2,1)S(1)}, bf16[64,1800]{1,0:T(8,128)(2,1)S(1)}, u32[]{:S(2)}, u32[]{:S(2)}) %collective-permute-start.4) | collective-permute-done | bytes 230432 | tf_op jit(solution)/shard_map/ppermute | solution.py:35
  40.1 1.5 %collective-permute-done.5 = bf16[64,1800]{1,0:T(8,128)(2,1)S(1)} collective-permute-done((bf16[64,1800]{1,0:T(8,128)(2,1)S(1)}, bf16[64,1800]{1,0:T(8,128)(2,1)S(1)}, u32[]{:S(2)}, u32[]{:S(2)}) %collective-permute-start.5) | collective-permute-done | bytes 230432 | tf_op jit(solution)/shard_map/ppermute | solution.py:35
  41.8 1.3 %collective-permute-start.21 = (bf16[64,900]{1,0:T(8,128)(2,1)S(1)}, bf16[64,900]{1,0:T(8,128)(2,1)S(1)}, u32[]{:S(2)}, u32[]{:S(2)}) collective-permute-start(bf16[64,900]{1,0:T(8,128)(2,1)S(1)} %get-tuple-element.17), channel_id=1, source_target_pairs={{0,64},{1,65},{2,81},{3,80},{4,32},{5,33},{6,49},{7,48},{8,0},{9,1... | collective-permute-start | bytes 345608 | tf_op jit(solution)/shard_map/ppermute | solution.py:35
  43.2 1.7 %collective-permute-start.22 = (bf16[64,900]{1,0:T(8,128)(2,1)S(1)}, bf16[64,900]{1,0:T(8,128)(2,1)S(1)}, u32[]{:S(2)}, u32[]{:S(2)}) collective-permute-start(bf16[64,900]{1,0:T(8,128)(2,1)S(1)} %get-tuple-element.18), channel_id=1, source_target_pairs={{0,81},{1,80},{2,64},{3,65},{4,49},{5,48},{6,32},{7,33},{8,17},{9,... | collective-permute-start | bytes 345608 | tf_op jit(solution)/shard_map/ppermute | solution.py:35
  44.8 5.2 %collective-permute-start.13 = (bf16[64,1800]{1,0:T(8,128)(2,1)S(1)}, bf16[64,1800]{1,0:T(8,128)(2,1)S(1)}, u32[]{:S(2)}, u32[]{:S(2)}) collective-permute-start(bf16[64,1800]{1,0:T(8,128)(2,1)S(1)} %select_convert_fusion.refs_0_), channel_id=1, source_target_pairs={{0,2},{1,3},{2,0},{3,1},{4,6},{5,7},{6,4},{7,5},{8,10},{9,11},{10,... | collective-permute-start | bytes 691208 | tf_op jit(solution)/shard_map/ppermute | solution.py:35
  50.0 3.3 %collective-permute-start.11 = (bf16[64,1800]{1,0:T(8,128)(2,1)S(1)}, bf16[64,1800]{1,0:T(8,128)(2,1)S(1)}, u32[]{:S(2)}, u32[]{:S(2)}) collective-permute-start(bf16[64,1800]{1,0:T(8,128)(2,1)S(1)} %select_convert_fusion.refs_0_), channel_id=1, source_target_pairs={{0,12},{1,13},{2,14},{3,15},{4,0},{5,1},{6,2},{7,3},{8,4},{9,5},{1... | collective-permute-start | bytes 691208 | tf_op jit(solution)/shard_map/ppermute | solution.py:35
  54.0 4.2 %collective-permute-start.28 = (bf16[2,64,900]{2,1,0:T(8,128)(2,1)S(1)}, bf16[2,64,900]{2,1,0:T(8,128)(2,1)S(1)}, u32[]{:S(2)}, u32[]{:S(2)}) collective-permute-start(bf16[2,64,900]{2,1,0:T(8,128)(2,1)S(1)} %pad_maximum_fusion.refs_16_), channel_id=1, source_target_pairs={{0,96},{1,97},{2,98},{3,99},{4,100},{5,101},{6,102},{7,103},{8,104... | collective-permute-start | bytes 691208 | tf_op jit(solution)/shard_map/ppermute | solution.py:35
  58.2 5.8 %collective-permute-done.11.refs_6_ = bf16[64,1800]{1,0:T(8,128)(2,1)S(1)} collective-permute-done((bf16[64,1800]{1,0:T(8,128)(2,1)S(1)}, bf16[64,1800]{1,0:T(8,128)(2,1)S(1)}, u32[]{:S(2)}, u32[]{:S(2)}) %collective-permute-start.11) | collective-permute-done | bytes 230432 | tf_op jit(solution)/shard_map/ppermute | solution.py:35
  63.9 3.5 %collective-permute-done.7.refs_2_ = bf16[64,1800]{1,0:T(8,128)(2,1)S(1)} collective-permute-done((bf16[64,1800]{1,0:T(8,128)(2,1)S(1)}, bf16[64,1800]{1,0:T(8,128)(2,1)S(1)}, u32[]{:S(2)}, u32[]{:S(2)}) %collective-permute-start.7) | collective-permute-done | bytes 230432 | tf_op jit(solution)/shard_map/ppermute | solution.py:35
  70.3 2.2 %collective-permute-done.26.refs_20_ = bf16[2,64,900]{2,1,0:T(8,128)(2,1)S(1)} collective-permute-done((bf16[2,64,900]{2,1,0:T(8,128)(2,1)S(1)}, bf16[2,64,900]{2,1,0:T(8,128)(2,1)S(1)}, u32[]{:S(2)}, u32[]{:S(2)}) %collective-permute-start.26) | collective-permute-done | bytes 230432 | tf_op jit(solution)/shard_map/ppermute | solution.py:35
  72.5 6.2 %collective-permute-done.24.refs_18_ = bf16[2,64,900]{2,1,0:T(8,128)(2,1)S(1)} collective-permute-done((bf16[2,64,900]{2,1,0:T(8,128)(2,1)S(1)}, bf16[2,64,900]{2,1,0:T(8,128)(2,1)S(1)}, u32[]{:S(2)}, u32[]{:S(2)}) %collective-permute-start.24) | collective-permute-done | bytes 230432 | tf_op jit(solution)/shard_map/ppermute | solution.py:35
  79.5 3.5 %collective-permute-start.12 = (bf16[64,1800]{1,0:T(8,128)(2,1)S(1)}, bf16[64,1800]{1,0:T(8,128)(2,1)S(1)}, u32[]{:S(2)}, u32[]{:S(2)}) collective-permute-start(bf16[64,1800]{1,0:T(8,128)(2,1)S(1)} %collective-permute-done.6.refs_1_), channel_id=1, source_target_pairs={{0,12},{1,13},{2,14},{3,15},{4,0},{5,1},{6,2},{7,3},{8,4},{9,5},{1... | collective-permute-start | bytes 691208 | tf_op jit(solution)/shard_map/ppermute | solution.py:35
  83.0 2.4 %collective-permute-start.27 = (bf16[2,64,900]{2,1,0:T(8,128)(2,1)S(1)}, bf16[2,64,900]{2,1,0:T(8,128)(2,1)S(1)}, u32[]{:S(2)}, u32[]{:S(2)}) collective-permute-start(bf16[2,64,900]{2,1,0:T(8,128)(2,1)S(1)} %collective-permute-done.26.refs_20_), channel_id=1, source_target_pairs={{0,16},{1,17},{2,18},{3,19},{4,20},{5,21},{6,22},{7,23},{8,24},{9,... | collective-permute-start | bytes 691208 | tf_op jit(solution)/shard_map/ppermute | solution.py:35
  87.8 1.3 %collective-permute-start.18 = (bf16[64,1800]{1,0:T(8,128)(2,1)S(1)}, bf16[64,1800]{1,0:T(8,128)(2,1)S(1)}, u32[]{:S(2)}, u32[]{:S(2)}) collective-permute-start(bf16[64,1800]{1,0:T(8,128)(2,1)S(1)} %collective-permute-done.10.refs_5_), channel_id=1, source_target_pairs={{0,2},{1,3},{2,0},{3,1},{4,6},{5,7},{6,4},{7,5},{8,10},{9,11},{10,... | collective-permute-start | bytes 691208 | tf_op jit(solution)/shard_map/ppermute | solution.py:35
  89.1 1.8 %collective-permute-done.8.refs_3_ = bf16[64,1800]{1,0:T(8,128)(2,1)S(1)} collective-permute-done((bf16[64,1800]{1,0:T(8,128)(2,1)S(1)}, bf16[64,1800]{1,0:T(8,128)(2,1)S(1)}, u32[]{:S(2)}, u32[]{:S(2)}) %collective-permute-start.8) | collective-permute-done | bytes 230432 | tf_op jit(solution)/shard_map/ppermute | solution.py:35
  91.0 1.6 %collective-permute-start.20 = (bf16[64,1800]{1,0:T(8,128)(2,1)S(1)}, bf16[64,1800]{1,0:T(8,128)(2,1)S(1)}, u32[]{:S(2)}, u32[]{:S(2)}) collective-permute-start(bf16[64,1800]{1,0:T(8,128)(2,1)S(1)} %collective-permute-done.12.refs_7_), channel_id=1, source_target_pairs={{0,2},{1,3},{2,0},{3,1},{4,6},{5,7},{6,4},{7,5},{8,10},{9,11},{10,... | collective-permute-start | bytes 691208 | tf_op jit(solution)/shard_map/ppermute | solution.py:35
  94.4 5.0 %product.1 = bf16[900,1800]{1,0:T(8,128)(2,1)} custom-call(bf16[64,1800]{1,0:T(8,128)(2,1)S(1)} %select_convert_fusion.refs_0_, bf16[64,1800]{1,0:T(8,128)(2,1)S(1)} %collective-permute-done.6.refs_1_, bf16[64,1800]{1,0:T(8,128)(2,1)S(1)} %collective-permute-done.7.refs_2_, bf16[64,1800]{1,0:T(8,128)(2,1)S(1)} %collective-permute-done.8.refs_3_, ...), custom_call_target="tpu_custom_call" | custom-call | tf_op jit(solution)/shard_map/product/pallas_call | solution.py:231
  (44 shorter events, 10.0 us)
Async XLA Ops:
  13.2 10.2 %collective-permute-start = (bf16[2,64,1800]{2,1,0:T(8,128)(2,1)S(1)}, bf16[2,64,1800]{2,1,0:T(8,128)(2,1)S(1)}, u32[]{:S(2)}, u32[]{:S(2)}) collective-permute-start(bf16[2,64,1800]{2,1,0:T(8,128)(2,1)S(1)} %get-tuple-element.10), channel_id=1, source_target_pairs={{0,64},{1,65},{2,18},{3,19},{4,68},{5,69},{6,22},{7,23},{8,72},{9,... | collective-permute-start | bytes 1382408 | tf_op jit(solution)/shard_map/ppermute | solution.py:35
  16.9 11.5 %collective-permute-start.1 = (bf16[2,64,1800]{2,1,0:T(8,128)(2,1)S(1)}, bf16[2,64,1800]{2,1,0:T(8,128)(2,1)S(1)}, u32[]{:S(2)}, u32[]{:S(2)}) collective-permute-start(bf16[2,64,1800]{2,1,0:T(8,128)(2,1)S(1)} %get-tuple-element.11), channel_id=1, source_target_pairs={{0,32},{1,33},{2,18},{3,19},{4,36},{5,37},{6,22},{7,23},{8,40},{9,... | collective-permute-start | bytes 1382408 | tf_op jit(solution)/shard_map/ppermute | solution.py:35
  16.9 11.4 %collective-permute-start.2 = (bf16[2,64,1800]{2,1,0:T(8,128)(2,1)S(1)}, bf16[2,64,1800]{2,1,0:T(8,128)(2,1)S(1)}, u32[]{:S(2)}, u32[]{:S(2)}) collective-permute-start(bf16[2,64,1800]{2,1,0:T(8,128)(2,1)S(1)} %get-tuple-element.12), channel_id=1, source_target_pairs={{0,96},{1,97},{2,2},{3,3},{4,100},{5,101},{6,6},{7,7},{8,104},{9,1... | collective-permute-start | bytes 1382408 | tf_op jit(solution)/shard_map/ppermute | solution.py:35
  28.8 9.7 %collective-permute-start.3 = (bf16[64,1800]{1,0:T(8,128)(2,1)S(1)}, bf16[64,1800]{1,0:T(8,128)(2,1)S(1)}, u32[]{:S(2)}, u32[]{:S(2)}) collective-permute-start(bf16[64,1800]{1,0:T(8,128)(2,1)S(1)} %fusion.4), channel_id=1, source_target_pairs={{0,16},{1,17},{2,66},{3,67},{4,20},{5,21},{6,70},{7,71},{8,24},{9,... | collective-permute-start | bytes 691208 | tf_op jit(solution)/shard_map/ppermute | solution.py:35
  32.0 8.1 %collective-permute-start.4 = (bf16[64,1800]{1,0:T(8,128)(2,1)S(1)}, bf16[64,1800]{1,0:T(8,128)(2,1)S(1)}, u32[]{:S(2)}, u32[]{:S(2)}) collective-permute-start(bf16[64,1800]{1,0:T(8,128)(2,1)S(1)} %get-tuple-element.13), channel_id=1, source_target_pairs={{0,0},{1,1},{2,34},{3,35},{4,4},{5,5},{6,38},{7,39},{8,8},{9,9},{1... | collective-permute-start | bytes 691208 | tf_op jit(solution)/shard_map/ppermute | solution.py:35
  41.8 11.5 %collective-permute-start.21 = (bf16[64,900]{1,0:T(8,128)(2,1)S(1)}, bf16[64,900]{1,0:T(8,128)(2,1)S(1)}, u32[]{:S(2)}, u32[]{:S(2)}) collective-permute-start(bf16[64,900]{1,0:T(8,128)(2,1)S(1)} %get-tuple-element.17), channel_id=1, source_target_pairs={{0,64},{1,65},{2,81},{3,80},{4,32},{5,33},{6,49},{7,48},{8,0},{9,1... | collective-permute-start | bytes 345608 | tf_op jit(solution)/shard_map/ppermute | solution.py:35
  43.2 10.8 %collective-permute-start.22 = (bf16[64,900]{1,0:T(8,128)(2,1)S(1)}, bf16[64,900]{1,0:T(8,128)(2,1)S(1)}, u32[]{:S(2)}, u32[]{:S(2)}) collective-permute-start(bf16[64,900]{1,0:T(8,128)(2,1)S(1)} %get-tuple-element.18), channel_id=1, source_target_pairs={{0,81},{1,80},{2,64},{3,65},{4,49},{5,48},{6,32},{7,33},{8,17},{9,... | collective-permute-start | bytes 345608 | tf_op jit(solution)/shard_map/ppermute | solution.py:35
  44.8 9.1 %collective-permute-start.13 = (bf16[64,1800]{1,0:T(8,128)(2,1)S(1)}, bf16[64,1800]{1,0:T(8,128)(2,1)S(1)}, u32[]{:S(2)}, u32[]{:S(2)}) collective-permute-start(bf16[64,1800]{1,0:T(8,128)(2,1)S(1)} %select_convert_fusion.refs_0_), channel_id=1, source_target_pairs={{0,2},{1,3},{2,0},{3,1},{4,6},{5,7},{6,4},{7,5},{8,10},{9,11},{10,... | collective-permute-start | bytes 691208 | tf_op jit(solution)/shard_map/ppermute | solution.py:35
  50.0 13.9 %collective-permute-start.11 = (bf16[64,1800]{1,0:T(8,128)(2,1)S(1)}, bf16[64,1800]{1,0:T(8,128)(2,1)S(1)}, u32[]{:S(2)}, u32[]{:S(2)}) collective-permute-start(bf16[64,1800]{1,0:T(8,128)(2,1)S(1)} %select_convert_fusion.refs_0_), channel_id=1, source_target_pairs={{0,12},{1,13},{2,14},{3,15},{4,0},{5,1},{6,2},{7,3},{8,4},{9,5},{1... | collective-permute-start | bytes 691208 | tf_op jit(solution)/shard_map/ppermute | solution.py:35
  53.3 10.6 %collective-permute-start.9 = (bf16[64,1800]{1,0:T(8,128)(2,1)S(1)}, bf16[64,1800]{1,0:T(8,128)(2,1)S(1)}, u32[]{:S(2)}, u32[]{:S(2)}) collective-permute-start(bf16[64,1800]{1,0:T(8,128)(2,1)S(1)} %select_convert_fusion.refs_0_), channel_id=1, source_target_pairs={{0,8},{1,9},{2,10},{3,11},{4,12},{5,13},{6,14},{7,15},{8,0},{9,1},... | collective-permute-start | bytes 691208 | tf_op jit(solution)/shard_map/ppermute | solution.py:35
  53.3 14.1 %collective-permute-start.7 = (bf16[64,1800]{1,0:T(8,128)(2,1)S(1)}, bf16[64,1800]{1,0:T(8,128)(2,1)S(1)}, u32[]{:S(2)}, u32[]{:S(2)}) collective-permute-start(bf16[64,1800]{1,0:T(8,128)(2,1)S(1)} %select_convert_fusion.refs_0_), channel_id=1, source_target_pairs={{0,4},{1,5},{2,6},{3,7},{4,8},{5,9},{6,10},{7,11},{8,12},{9,13},{1... | collective-permute-start | bytes 691208 | tf_op jit(solution)/shard_map/ppermute | solution.py:35
  53.9 14.3 %collective-permute-start.6 = (bf16[64,1800]{1,0:T(8,128)(2,1)S(1)}, bf16[64,1800]{1,0:T(8,128)(2,1)S(1)}, u32[]{:S(2)}, u32[]{:S(2)}) collective-permute-start(bf16[64,1800]{1,0:T(8,128)(2,1)S(1)} %select_convert_fusion.refs_0_), channel_id=1, source_target_pairs={{0,1},{1,0},{2,3},{3,2},{4,5},{5,4},{6,7},{7,6},{8,9},{9,8},{10,11... | collective-permute-start | bytes 691208 | tf_op jit(solution)/shard_map/ppermute | solution.py:35
  54.0 15.6 %collective-permute-start.28 = (bf16[2,64,900]{2,1,0:T(8,128)(2,1)S(1)}, bf16[2,64,900]{2,1,0:T(8,128)(2,1)S(1)}, u32[]{:S(2)}, u32[]{:S(2)}) collective-permute-start(bf16[2,64,900]{2,1,0:T(8,128)(2,1)S(1)} %pad_maximum_fusion.refs_16_), channel_id=1, source_target_pairs={{0,96},{1,97},{2,98},{3,99},{4,100},{5,101},{6,102},{7,103},{8,104... | collective-permute-start | bytes 691208 | tf_op jit(solution)/shard_map/ppermute | solution.py:35
  63.9 8.6 %collective-permute-start.26 = (bf16[2,64,900]{2,1,0:T(8,128)(2,1)S(1)}, bf16[2,64,900]{2,1,0:T(8,128)(2,1)S(1)}, u32[]{:S(2)}, u32[]{:S(2)}) collective-permute-start(bf16[2,64,900]{2,1,0:T(8,128)(2,1)S(1)} %pad_maximum_fusion.refs_16_), channel_id=1, source_target_pairs={{0,64},{1,65},{2,66},{3,67},{4,68},{5,69},{6,70},{7,71},{8,72},{9,... | collective-permute-start | bytes 691208 | tf_op jit(solution)/shard_map/ppermute | solution.py:35
  63.9 14.8 %collective-permute-start.24 = (bf16[2,64,900]{2,1,0:T(8,128)(2,1)S(1)}, bf16[2,64,900]{2,1,0:T(8,128)(2,1)S(1)}, u32[]{:S(2)}, u32[]{:S(2)}) collective-permute-start(bf16[2,64,900]{2,1,0:T(8,128)(2,1)S(1)} %pad_maximum_fusion.refs_16_), channel_id=1, source_target_pairs={{0,32},{1,33},{2,34},{3,35},{4,36},{5,37},{6,38},{7,39},{8,40},{9,... | collective-permute-start | bytes 691208 | tf_op jit(solution)/shard_map/ppermute | solution.py:35
  67.4 12.1 %collective-permute-start.23 = (bf16[2,64,900]{2,1,0:T(8,128)(2,1)S(1)}, bf16[2,64,900]{2,1,0:T(8,128)(2,1)S(1)}, u32[]{:S(2)}, u32[]{:S(2)}) collective-permute-start(bf16[2,64,900]{2,1,0:T(8,128)(2,1)S(1)} %pad_maximum_fusion.refs_16_), channel_id=1, source_target_pairs={{0,16},{1,17},{2,18},{3,19},{4,20},{5,21},{6,22},{7,23},{8,24},{9,... | collective-permute-start | bytes 691208 | tf_op jit(solution)/shard_map/ppermute | solution.py:35
  68.3 11.2 %collective-permute-start.19 = (bf16[64,1800]{1,0:T(8,128)(2,1)S(1)}, bf16[64,1800]{1,0:T(8,128)(2,1)S(1)}, u32[]{:S(2)}, u32[]{:S(2)}) collective-permute-start(bf16[64,1800]{1,0:T(8,128)(2,1)S(1)} %collective-permute-done.11.refs_6_), channel_id=1, source_target_pairs={{0,2},{1,3},{2,0},{3,1},{4,6},{5,7},{6,4},{7,5},{8,10},{9,11},{10,... | collective-permute-start | bytes 691208 | tf_op jit(solution)/shard_map/ppermute | solution.py:35
  69.6 13.4 %collective-permute-start.17 = (bf16[64,1800]{1,0:T(8,128)(2,1)S(1)}, bf16[64,1800]{1,0:T(8,128)(2,1)S(1)}, u32[]{:S(2)}, u32[]{:S(2)}) collective-permute-start(bf16[64,1800]{1,0:T(8,128)(2,1)S(1)} %collective-permute-done.9.refs_4_), channel_id=1, source_target_pairs={{0,2},{1,3},{2,0},{3,1},{4,6},{5,7},{6,4},{7,5},{8,10},{9,11},{10,... | collective-permute-start | bytes 691208 | tf_op jit(solution)/shard_map/ppermute | solution.py:35
  72.5 10.5 %collective-permute-start.10 = (bf16[64,1800]{1,0:T(8,128)(2,1)S(1)}, bf16[64,1800]{1,0:T(8,128)(2,1)S(1)}, u32[]{:S(2)}, u32[]{:S(2)}) collective-permute-start(bf16[64,1800]{1,0:T(8,128)(2,1)S(1)} %collective-permute-done.9.refs_4_), channel_id=1, source_target_pairs={{0,1},{1,0},{2,3},{3,2},{4,5},{5,4},{6,7},{7,6},{8,9},{9,8},{10,11... | collective-permute-start | bytes 691208 | tf_op jit(solution)/shard_map/ppermute | solution.py:35
  79.5 8.4 %collective-permute-start.12 = (bf16[64,1800]{1,0:T(8,128)(2,1)S(1)}, bf16[64,1800]{1,0:T(8,128)(2,1)S(1)}, u32[]{:S(2)}, u32[]{:S(2)}) collective-permute-start(bf16[64,1800]{1,0:T(8,128)(2,1)S(1)} %collective-permute-done.6.refs_1_), channel_id=1, source_target_pairs={{0,12},{1,13},{2,14},{3,15},{4,0},{5,1},{6,2},{7,3},{8,4},{9,5},{1... | collective-permute-start | bytes 691208 | tf_op jit(solution)/shard_map/ppermute | solution.py:35
  83.0 8.0 %collective-permute-start.8 = (bf16[64,1800]{1,0:T(8,128)(2,1)S(1)}, bf16[64,1800]{1,0:T(8,128)(2,1)S(1)}, u32[]{:S(2)}, u32[]{:S(2)}) collective-permute-start(bf16[64,1800]{1,0:T(8,128)(2,1)S(1)} %collective-permute-done.6.refs_1_), channel_id=1, source_target_pairs={{0,4},{1,5},{2,6},{3,7},{4,8},{5,9},{6,10},{7,11},{8,12},{9,13},{1... | collective-permute-start | bytes 691208 | tf_op jit(solution)/shard_map/ppermute | solution.py:35
  83.0 9.6 %collective-permute-start.27 = (bf16[2,64,900]{2,1,0:T(8,128)(2,1)S(1)}, bf16[2,64,900]{2,1,0:T(8,128)(2,1)S(1)}, u32[]{:S(2)}, u32[]{:S(2)}) collective-permute-start(bf16[2,64,900]{2,1,0:T(8,128)(2,1)S(1)} %collective-permute-done.26.refs_20_), channel_id=1, source_target_pairs={{0,16},{1,17},{2,18},{3,19},{4,20},{5,21},{6,22},{7,23},{8,24},{9,... | collective-permute-start | bytes 691208 | tf_op jit(solution)/shard_map/ppermute | solution.py:35
  85.4 7.9 %collective-permute-start.29 = (bf16[2,64,900]{2,1,0:T(8,128)(2,1)S(1)}, bf16[2,64,900]{2,1,0:T(8,128)(2,1)S(1)}, u32[]{:S(2)}, u32[]{:S(2)}) collective-permute-start(bf16[2,64,900]{2,1,0:T(8,128)(2,1)S(1)} %collective-permute-done.23.refs_17_), channel_id=1, source_target_pairs={{0,96},{1,97},{2,98},{3,99},{4,100},{5,101},{6,102},{7,103},{8,104... | collective-permute-start | bytes 691208 | tf_op jit(solution)/shard_map/ppermute | solution.py:35
  86.0 7.8 %collective-permute-start.25 = (bf16[2,64,900]{2,1,0:T(8,128)(2,1)S(1)}, bf16[2,64,900]{2,1,0:T(8,128)(2,1)S(1)}, u32[]{:S(2)}, u32[]{:S(2)}) collective-permute-start(bf16[2,64,900]{2,1,0:T(8,128)(2,1)S(1)} %collective-permute-done.23.refs_17_), channel_id=1, source_target_pairs={{0,32},{1,33},{2,34},{3,35},{4,36},{5,37},{6,38},{7,39},{8,40},{9,... | collective-permute-start | bytes 691208 | tf_op jit(solution)/shard_map/ppermute | solution.py:35
  (6 other events, 31.2 us)
